TPU v7x, 256 devices: a whole 4x4x8 slice. The times are simulated.
256 devices in a mesh: batch: 16 (over x, y_hi, core), space: 16 (over z, y_lo).
Axes of the slice: x: 4, y: 4 (y_hi: 2, y_lo: 2; y = y_hi * 2 + y_lo), z: 8, core: 2. Of those that a mesh axis runs over, the one named last changes fastest.
Arguments:
- snapshots: bfloat16 [16, 64, 32, 1024], P('batch', None, 'space'), may hold values from -6 to 6
- cotangent: bfloat16 [16, 64, 32, 1024], P('batch', None, 'space'), may hold values from -6 to 6
- mode_weight: bfloat16 [16, 16, 24, 64, 64], P('batch', 'space'), may hold values from -0.75 to 0.75
- conv_weight: bfloat16 [3, 3, 3, 64, 64], replicated, may hold values from -0.15625 to 0.15625
Outputs:
- activated: bfloat16 [16, 64, 32, 1024], P('batch', None, 'space')
- input_gradient: bfloat16 [16, 64, 32, 1024], P('batch', None, 'space')
- mode_gradient: float32 [16, 16, 24, 64, 64], P('batch', 'space')
- conv_gradient: float32 [3, 3, 3, 64, 64], replicated
All inputs are finite; a program needn't handle non-finite values.
Results may differ from a plain program's by a relative error of at most 0.02.
Values may be sent and summed in bfloat16 or wider, within the bound.
A program may use at most 128 MiB of HBM per device.

v0:
```python
import math
import jax
import jax.numpy as jnp
from jax import lax
from jax.sharding import PartitionSpec as P

KX = 8
KY = 8
KZ = 12
NX = 32
NY = 32
inv_root_two = 1.0 / math.sqrt(2.0)
inv_root_two_pi = 1.0 / math.sqrt(2.0 * math.pi)


def extended_2(cells, sides, width):
    for axis, dim in sides:
        count = lax.axis_size(axis)
        ends = count - 1
        head = lax.slice_in_dim(cells, 0, width, axis=dim)
        tail = lax.slice_in_dim(cells, cells.shape[dim] - width, cells.shape[dim], axis=dim)
        cells = jnp.concatenate(
            [
                lax.ppermute(tail, axis, [(i, (i + 1) % count) for i in range(ends)]),
                cells,
                lax.ppermute(head, axis, [((i + 1) % count, i) for i in range(ends)]),
            ],
            axis=dim,
        )
    return cells


def basis_rows(half_count, length):
    row_index = lax.broadcasted_iota(jnp.int32, (2 * half_count, length), 0)
    cell_index = lax.broadcasted_iota(jnp.int32, (2 * half_count, length), 1)
    frequency = jnp.where(row_index < half_count, row_index, row_index - half_count + 1)
    phases = (frequency * cell_index % length).astype(jnp.float32) * (2.0 * math.pi / length)
    return jnp.where(row_index < half_count, jnp.cos(phases), jnp.sin(phases))


def make_tables(count_x, count_y, count_z, length_x, length_y, length_z):
    across = basis_rows(count_x, length_x)
    along_y = basis_rows(count_y, length_y)
    depth_rows = basis_rows(count_z, length_z)
    modes_x = 2 * count_x
    modes_y = 2 * count_y
    outer_table = (across[:, None, :, None] * along_y[None, :, None, :]).reshape(
        modes_x * modes_y, length_x * length_y
    )
    plane_analysis = (outer_table * (2.0 / math.sqrt(length_x * length_y))).astype(jnp.bfloat16)
    plane_synthesis = (outer_table.T * (2.0 / math.sqrt(modes_x * modes_y))).astype(jnp.bfloat16)
    depth_analysis = (depth_rows * math.sqrt(2.0 / length_z)).astype(jnp.bfloat16)
    depth_synthesis = (depth_rows.T * math.sqrt(2.0 / (2 * count_z))).astype(jnp.bfloat16)
    return (plane_analysis, plane_synthesis, depth_analysis, depth_synthesis)


def rim(values):
    return extended_2(values, (("space", 1),), 1)


def widen(values):
    channels, depth_cells, plane = values.shape
    extended = rim(values)
    return jnp.pad(
        extended.reshape(channels, depth_cells + 2, NX, NY), ((0, 0), (0, 0), (1, 1), (1, 1))
    )


def to_pencils(values):
    return lax.all_to_all(values, "space", split_axis=3, concat_axis=1, tiled=True)


def to_slabs(values):
    return lax.all_to_all(values, "space", split_axis=1, concat_axis=3, tiled=True)


def stacked_window(padded, offset_x, offset_y):
    channels = padded.shape[0]
    depth_cells = padded.shape[1] - 2
    window = padded[:, :, offset_x : offset_x + NX, offset_y : offset_y + NY]
    stacked = jnp.stack([window[:, offset_z : offset_z + depth_cells] for offset_z in range(3)], 0)
    return stacked.reshape(3, channels, depth_cells * NX * NY)


def stencil(padded, kernel):
    depth_cells = padded.shape[1] - 2
    summed = jnp.zeros((kernel.shape[4], depth_cells * NX * NY), jnp.float32)
    for offset_x in range(3):
        for offset_y in range(3):
            stacked = stacked_window(padded, offset_x, offset_y)
            summed = summed + lax.dot_general(
                kernel[:, offset_x, offset_y],
                stacked,
                (((0, 1), (0, 1)), ((), ())),
                preferred_element_type=jnp.float32,
            )
    return summed


def kernel_terms(padded, pre_flat):
    pieces = []
    for offset_x in range(3):
        row_pieces = []
        for offset_y in range(3):
            stacked = stacked_window(padded, offset_x, offset_y)
            row_pieces.append(
                lax.dot_general(
                    stacked, pre_flat, (((2,), (1,)), ((), ())), preferred_element_type=jnp.float32
                )
            )
        pieces.append(jnp.stack(row_pieces, 1))
    return jnp.stack(pieces, 1)


def shards(snapshots, cotangent, mode_weight, conv_weight):
    local_field = snapshots[0]
    channels, depth_cells, plane = local_field.shape
    total_depth = depth_cells * lax.axis_size("space")
    modes_x = 2 * KX
    modes_y = 2 * KY
    plane_analysis, plane_synthesis, depth_analysis, depth_synthesis = make_tables(
        KX, KY, KZ, NX, NY, total_depth
    )
    padded = widen(local_field)
    plane_coef = lax.dot_general(
        local_field.reshape(channels * depth_cells, plane),
        plane_analysis,
        (((1,), (1,)), ((), ())),
        preferred_element_type=jnp.float32,
    )
    plane_coef = plane_coef.astype(jnp.bfloat16).reshape(channels, depth_cells, modes_x, modes_y)
    coef = jnp.einsum(
        "czxy,pz->cpxy", to_pencils(plane_coef), depth_analysis, preferred_element_type=jnp.float32
    ).astype(jnp.bfloat16)
    full_weight = lax.all_gather(mode_weight, "batch", axis=0, tiled=True)
    mixed = jnp.einsum(
        "ipxy,xypio->opxy", coef, full_weight, preferred_element_type=jnp.float32
    ).astype(jnp.bfloat16)
    depth_back = jnp.einsum(
        "opxy,zp->ozxy", mixed, depth_synthesis, preferred_element_type=jnp.float32
    ).astype(jnp.bfloat16)
    slab_back = to_slabs(depth_back)
    spectral = lax.dot_general(
        slab_back.reshape(channels * depth_cells, modes_x * modes_y),
        plane_synthesis,
        (((1,), (1,)), ((), ())),
        preferred_element_type=jnp.float32,
    )
    pre = spectral.reshape(channels, depth_cells * plane) + stencil(padded, conv_weight)
    normal_cdf = 0.5 * (1.0 + lax.erf(pre * inv_root_two))
    density = jnp.exp(-0.5 * pre * pre) * inv_root_two_pi
    activated = (pre * normal_cdf).astype(jnp.bfloat16).reshape(channels, depth_cells, plane)
    pre_grad = (
        cotangent[0].reshape(channels, depth_cells * plane).astype(jnp.float32)
        * (normal_cdf + pre * density)
    ).astype(jnp.bfloat16)
    back_plane = jnp.dot(
        pre_grad.reshape(channels * depth_cells, plane),
        plane_synthesis,
        preferred_element_type=jnp.float32,
    )
    back_plane = back_plane.astype(jnp.bfloat16).reshape(channels, depth_cells, modes_x, modes_y)
    mixed_grad = jnp.einsum(
        "ozxy,zp->opxy", to_pencils(back_plane), depth_synthesis, preferred_element_type=jnp.float32
    ).astype(jnp.bfloat16)
    coef_grad = jnp.einsum(
        "opxy,xypio->ipxy", mixed_grad, full_weight, preferred_element_type=jnp.float32
    ).astype(jnp.bfloat16)
    mode_gradient = lax.psum_scatter(
        jnp.einsum("ipxy,opxy->xypio", coef, mixed_grad, preferred_element_type=jnp.float32).astype(
            jnp.bfloat16
        ),
        "batch",
        scatter_dimension=0,
        tiled=True,
    ).astype(jnp.float32)
    depth_grad = jnp.einsum(
        "ipxy,pz->izxy", coef_grad, depth_analysis, preferred_element_type=jnp.float32
    ).astype(jnp.bfloat16)
    slab_grad = to_slabs(depth_grad)
    spectral_grad = jnp.dot(
        slab_grad.reshape(channels * depth_cells, modes_x * modes_y),
        plane_analysis,
        preferred_element_type=jnp.float32,
    )
    flipped = jnp.transpose(conv_weight[::-1, ::-1, ::-1], (0, 1, 2, 4, 3))
    local_grad = stencil(widen(pre_grad.reshape(channels, depth_cells, plane)), flipped)
    input_gradient = (
        (spectral_grad.reshape(channels, depth_cells * plane) + local_grad)
        .astype(jnp.bfloat16)
        .reshape(channels, depth_cells, plane)
    )
    kernel_local = kernel_terms(padded, pre_grad)
    kernel_total = lax.psum(kernel_local, ("batch", "space"))
    conv_gradient = kernel_total / math.sqrt(lax.axis_size("batch") * total_depth * plane)
    return (activated[None], input_gradient[None], mode_gradient, conv_gradient)


def solution(mesh):
    in_specs = (
        P("batch", None, "space", None),
        P("batch", None, "space", None),
        P("batch", "space", None, None, None),
        P(),
    )
    out_specs = (
        P("batch", None, "space", None),
        P("batch", None, "space", None),
        P("batch", "space", None, None, None),
        P(),
    )
    return jax.shard_map(shards, mesh=mesh, in_specs=in_specs, out_specs=out_specs, check_vma=False)
```

profile of v0, /device:TPU:2, one launch (start us, length us, event | category | flops | bytes accessed | tf_op | source)
XLA Modules:
  0.0 513.8 jit_solution(1458009510099474854)
XLA Ops:
  10.0 4.2 collective-permute-start
  15.5 1.8 reshape_squeeze.4
  17.4 2.2 fusion.6
  19.5 3.6 convert_element_type.165
  25.6 1.8 copy.99
  28.2 11.5 %all-to-all-start = ((bf16[16,2,1024]{2,1,0:T(2,128)(2,1)}), bf16[16,2,1024]{2,1,0:T(2,128)(2,1)S(1)}, u32[]{:S(2)}, u32[]{:S(2)}) async-start(bf16[16,2,1024]{2,1,0:T(2,128)(2,1)} %reshape.401), calls=%async_computation | async-start | bytes 131072 | tf_op jit(solution)/shard_map/all_to_all | solution.py:70
  40.6 1.8 copy.190
  42.4 2.9 convert_element_type.178
  45.3 3.4 all-to-all-done
  53.0 1.6 select_maximum_fusion.2
  54.6 1.5 fusion.196
  56.1 1.9 copy.109
  58.0 1.9 copy.107
  61.8 3.9 fusion.195
  65.7 2.0 copy.134
  67.7 2.0 copy.133
  69.7 1.9 copy.132
  71.6 1.9 copy.130
  73.6 1.9 copy.129
  75.5 1.9 copy.128
  77.5 1.9 copy.126
  81.2 2.0 copy.119
  83.2 2.0 copy.118
  85.2 1.9 copy.117
  87.1 1.9 copy.115
  89.0 1.9 copy.114
  93.7 1.4 convolution_bitcast_fusion.17
  95.2 1.5 fusion.19
  99.4 4.6 fusion.3
  105.2 5.1 %all-to-all-start.1 = ((bf16[16,2,1024]{2,1,0:T(2,128)(2,1)}), bf16[16,2,1024]{2,1,0:T(2,128)(2,1)}, u32[]{:S(2)}, u32[]{:S(2)}) async-start(bf16[16,2,1024]{2,1,0:T(2,128)(2,1)} %reshape.403), calls=%async_computation.1 | async-start | bytes 131072 | tf_op jit(solution)/shard_map/all_to_all | solution.py:74
  110.3 2.4 fusion.13
  115.5 3.9 all-to-all-done.1
  122.1 2.6 fusion.85
  124.7 2.1 convolution_bitcast_fusion.25
  136.7 4.3 all-to-all-start.2
  142.4 7.8 %all-to-all-done.2 = bf16[16,2,1024]{2,1,0:T(2,128)(2,1)S(1)} async-done(((bf16[16,2,1024]{2,1,0:T(2,128)(2,1)}), bf16[16,2,1024]{2,1,0:T(2,128)(2,1)S(1)}, u32[]{:S(2)}, u32[]{:S(2)}) %all-to-all-start.2) | async-done | bytes 65568 | tf_op jit(solution)/shard_map/all_to_all | solution.py:70
  150.7 5.8 %fusion = bf16[16,1,24,64,64]{4,3,2,1,0:T(8,128)(2,1)} fusion(f32[16,24,64]{2,1,0:T(8,128)S(1)} %get-tuple-element.76, f32[16,24,64]{2,1,0:T(8,128)S(1)} %get-tuple-element.77), kind=kLoop, calls=%fused_computation.1 | loop fusion | flops 3145728 | bytes 3342336 | tf_op jit(solution)/shard_map/convert_element_type | solution.py:170
  159.6 2.6 collective-permute-start.2
  162.2 1.3 collective-permute-start.3
  163.5 6.1 %fusion.1 = bf16[24,16,1,64]{3,2,1,0:T(2,128)(2,1)S(1)} fusion(bf16[64,24,16,1]{0,1,2,3:T(8,128)(2,1)S(1)} %bitcast.459, bf16[16,1,24,64,64]{4,3,2,1,0:T(8,128)(2,1)} %all-gather.2.cloned.1.call-done), kind=kOutput, calls=%fused_computation.4 | convolution fusion | flops 3145728 | bytes 3244032 | tf_op jit(solution)/shard_map/opxy,xypio->ipxy/dot_general | solution.py:166
  170.8 6.4 %all-to-all-start.3 = ((bf16[16,2,1024]{2,1,0:T(2,128)(2,1)}), bf16[16,2,1024]{2,1,0:T(2,128)(2,1)S(1)}, u32[]{:S(2)}, u32[]{:S(2)}) async-start(bf16[16,2,1024]{2,1,0:T(2,128)(2,1)} %reshape.407), calls=%async_computation.3 | async-start | bytes 131072 | tf_op jit(solution)/shard_map/all_to_all | solution.py:74
  179.3 1.6 select_maximum_fusion
  180.8 1.5 fusion.194
  182.3 2.0 copy.148
  184.3 1.9 copy.152
  188.9 3.8 fusion.193
  192.8 1.3 copy.147
  194.1 2.0 copy.172
  196.1 1.9 copy.171
  198.0 1.9 copy.170
  200.0 1.9 copy.169
  201.9 1.9 copy.168
  203.8 1.9 copy.167
  207.6 2.0 copy.164
  209.6 1.9 copy.163
  211.6 2.0 copy.162
  213.5 2.0 copy.159
  215.5 1.9 copy.158
  222.0 1.4 convolution_bitcast_fusion.4
  224.6 2.3 convolution_bitcast_fusion.1
  232.5 172.3 %all-reduce.4.cloned.1.call-done = f32[3,3,3,64,64]{4,3,0,2,1:T(8,128)} async-done(((f32[3,3,3,64,64]{4,3,0,2,1:T(8,128)}), f32[3,3,3,64,64]{4,3,0,2,1:T(8,128)}) %all-reduce.4.cloned.1.call-update) | async-done | bytes 442384 | tf_op jit(solution)/shard_map/psum | solution.py:194
  409.0 2.4 fusion.30
  412.3 92.8 %reduce-scatter.2.cloned.1.call-done = bf16[1,1,24,64,64]{4,3,2,1,0:T(8,128)(2,1)} async-done(((bf16[16,1,24,64,64]{4,3,2,1,0:T(8,128)(2,1)}), bf16[1,1,24,64,64]{4,3,2,1,0:T(8,128)(2,1)}) %reduce-scatter.2.cloned.1.call-update) | async-done | bytes 196624 | tf_op jit(solution)/shard_map/reduce_scatter | solution.py:169
  505.1 2.0 convert_element_type.196
  (293 shorter events, 66.7 us)
Async XLA Ops:
  7.2 92.2 %all-gather.2.cloned.1.call-start = ((), (), s32[]{:S(2)}) async-start(), calls=%async_computation.5 | async-start | bytes 6684672 | tf_op jit(solution)/shard_map/all_gather | solution.py:135
  10.0 40.0 %collective-permute-start = (bf16[64,1,1024]{0,2,1:T(8,128)(2,1)}, bf16[64,1,1024]{0,2,1:T(8,128)(2,1)}, u32[]{:S(2)}, u32[]{:S(2)}) collective-permute-start(bf16[64,1,1024]{0,2,1:T(8,128)(2,1)} %get-tuple-element.72), channel_id=1, source_target_pairs={{0,1},{1,2},{2,3},{3,4},{4,5},{5,6},{6,7},{7,8},{8,9},{9,10},{10,1... | collective-permute-start | bytes 393224 | tf_op jit(solution)/shard_map/ppermute | solution.py:24
  14.2 35.8 %collective-permute-start.1 = (bf16[64,1,1024]{0,2,1:T(8,128)(2,1)}, bf16[64,1,1024]{0,2,1:T(8,128)(2,1)}, u32[]{:S(2)}, u32[]{:S(2)}) collective-permute-start(bf16[64,1,1024]{0,2,1:T(8,128)(2,1)} %get-tuple-element.73), channel_id=1, source_target_pairs={{1,0},{2,1},{3,2},{4,3},{5,4},{6,5},{7,6},{8,7},{9,8},{10,9},{11,1... | collective-permute-start | bytes 393224 | tf_op jit(solution)/shard_map/ppermute | solution.py:26
  19.5 20.2 %copy-start.1 = (bf16[1,64,2,1024]{3,2,1,0:T(2,128)(2,1)S(1)}, bf16[1,64,2,1024]{3,2,1,0:T(2,128)(2,1)}, u32[]{:S(2)}) copy-start(bf16[1,64,2,1024]{3,2,1,0:T(2,128)(2,1)} %param.4) | copy-start | bytes 786436
  28.2 20.6 %all-to-all-start = ((bf16[16,2,1024]{2,1,0:T(2,128)(2,1)}), bf16[16,2,1024]{2,1,0:T(2,128)(2,1)S(1)}, u32[]{:S(2)}, u32[]{:S(2)}) async-start(bf16[16,2,1024]{2,1,0:T(2,128)(2,1)} %reshape.401), calls=%async_computation | async-start | bytes 131072 | tf_op jit(solution)/shard_map/all_to_all | solution.py:70
  65.7 13.7 %copy-start.9 = (bf16[64,2,32,32]{0,3,2,1:T(8,128)(2,1)S(1)}, bf16[64,2,32,32]{0,3,2,1:T(8,128)(2,1)}, u32[]{:S(2)}) copy-start(bf16[64,2,32,32]{0,3,2,1:T(8,128)(2,1)} %get-tuple-element.49) | copy-start | bytes 786436
  67.7 12.6 %copy-start.7 = (bf16[64,2,32,32]{0,3,2,1:T(8,128)(2,1)S(1)}, bf16[64,2,32,32]{0,3,2,1:T(8,128)(2,1)}, u32[]{:S(2)}) copy-start(bf16[64,2,32,32]{0,3,2,1:T(8,128)(2,1)} %get-tuple-element.50) | copy-start | bytes 786436
  80.3 11.6 %copy-start.5 = (bf16[64,2,32,32]{0,3,2,1:T(8,128)(2,1)S(1)}, bf16[64,2,32,32]{0,3,2,1:T(8,128)(2,1)}, u32[]{:S(2)}) copy-start(bf16[64,2,32,32]{0,3,2,1:T(8,128)(2,1)} %get-tuple-element.57) | copy-start | bytes 786436
  81.2 11.6 %copy-start.3 = (bf16[64,2,32,32]{0,3,2,1:T(8,128)(2,1)S(1)}, bf16[64,2,32,32]{0,3,2,1:T(8,128)(2,1)}, u32[]{:S(2)}) copy-start(bf16[64,2,32,32]{0,3,2,1:T(8,128)(2,1)} %get-tuple-element.58) | copy-start | bytes 786436
  83.2 10.5 %copy-start.22 = (bf16[1,64,2048]{2,1,0:T(8,128)(2,1)S(1)}, bf16[1,64,2048]{2,1,0:T(8,128)(2,1)}, u32[]{:S(2)}) copy-start(bf16[1,64,2048]{2,1,0:T(8,128)(2,1)} %copy.107) | copy-start | bytes 786436
  91.8 3.3 copy-start.19
  92.8 3.9 copy-start.55
  92.8 3.9 copy-start.57
  93.7 3.3 copy-start.49
  93.7 3.3 copy-start.51
  93.7 3.4 copy-start.53
  99.4 10.9 %copy-start.30 = (bf16[1,64,2048]{2,1,0:T(8,128)(2,1)S(1)}, bf16[1,64,2048]{2,1,0:T(8,128)(2,1)}, u32[]{:S(2)}) copy-start(bf16[1,64,2048]{2,1,0:T(8,128)(2,1)} %copy.134) | copy-start | bytes 786436
  99.4 10.9 %copy-start.32 = (bf16[1,64,2048]{2,1,0:T(8,128)(2,1)S(1)}, bf16[1,64,2048]{2,1,0:T(8,128)(2,1)}, u32[]{:S(2)}) copy-start(bf16[1,64,2048]{2,1,0:T(8,128)(2,1)} %copy.133) | copy-start | bytes 786436
  104.0 9.7 %copy-start.2 = (bf16[64,2,32,32]{0,3,2,1:T(8,128)(2,1)S(1)}, bf16[64,2,32,32]{0,3,2,1:T(8,128)(2,1)}, u32[]{:S(2)}) copy-start(bf16[64,2,32,32]{0,3,2,1:T(8,128)(2,1)} %get-tuple-element.40) | copy-start | bytes 786436
  105.2 14.2 %all-to-all-start.1 = ((bf16[16,2,1024]{2,1,0:T(2,128)(2,1)}), bf16[16,2,1024]{2,1,0:T(2,128)(2,1)}, u32[]{:S(2)}, u32[]{:S(2)}) async-start(bf16[16,2,1024]{2,1,0:T(2,128)(2,1)} %reshape.403), calls=%async_computation.1 | async-start | bytes 131072 | tf_op jit(solution)/shard_map/all_to_all | solution.py:74
  110.3 11.3 %copy-start = (bf16[256,1024]{1,0:T(8,128)(2,1)S(1)}, bf16[256,1024]{1,0:T(8,128)(2,1)}, u32[]{:S(2)}) copy-start(bf16[256,1024]{1,0:T(8,128)(2,1)} %convert_element_type.178) | copy-start | bytes 1572868
  113.6 8.5 %copy-start.18 = (f32[8,8,2,1024]{3,1,2,0:T(8,128)S(1)}, f32[8,8,2,1024]{3,1,2,0:T(8,128)}, u32[]{:S(2)}) copy-start(f32[8,8,2,1024]{3,1,2,0:T(8,128)} %copy.190) | copy-start | bytes 1572868
  122.1 4.7 copy-start.56
  122.1 4.7 copy-start.58
  122.1 4.7 copy-start.60
  124.7 33.7 %copy-start.13 = (bf16[64,2048]{1,0:T(8,128)(2,1)}, bf16[64,2048]{1,0:T(8,128)(2,1)S(1)}, u32[]{:S(2)}) copy-start(bf16[64,2048]{1,0:T(8,128)(2,1)S(1)} %get-tuple-element.68) | copy-start | bytes 786436
  124.7 3.2 copy-start.52
  124.7 3.2 copy-start.54
  134.1 7.0 %copy-start.88 = (f32[3,1,64,64]{3,2,0,1:T(8,128)S(1)}, f32[3,1,64,64]{3,2,0,1:T(8,128)}, u32[]{:S(2)}) copy-start(f32[3,1,64,64]{3,2,0,1:T(8,128)} %convolution_bitcast_fusion.20) | copy-start | bytes 147460
  134.1 7.0 %copy-start.89 = (f32[3,1,64,64]{3,2,0,1:T(8,128)S(1)}, f32[3,1,64,64]{3,2,0,1:T(8,128)}, u32[]{:S(2)}) copy-start(f32[3,1,64,64]{3,2,0,1:T(8,128)} %convolution_bitcast_fusion.19) | copy-start | bytes 147460
  134.1 7.1 %copy-start.83 = (f32[3,1,64,64]{3,2,0,1:T(8,128)S(1)}, f32[3,1,64,64]{3,2,0,1:T(8,128)}, u32[]{:S(2)}) copy-start(f32[3,1,64,64]{3,2,0,1:T(8,128)} %convolution_bitcast_fusion.25) | copy-start | bytes 147460
  134.1 7.1 %copy-start.84 = (f32[3,1,64,64]{3,2,0,1:T(8,128)S(1)}, f32[3,1,64,64]{3,2,0,1:T(8,128)}, u32[]{:S(2)}) copy-start(f32[3,1,64,64]{3,2,0,1:T(8,128)} %convolution_bitcast_fusion.24) | copy-start | bytes 147460
  134.1 7.1 %copy-start.85 = (f32[3,1,64,64]{3,2,0,1:T(8,128)S(1)}, f32[3,1,64,64]{3,2,0,1:T(8,128)}, u32[]{:S(2)}) copy-start(f32[3,1,64,64]{3,2,0,1:T(8,128)} %convolution_bitcast_fusion.23) | copy-start | bytes 147460
  134.1 7.1 %copy-start.86 = (f32[3,1,64,64]{3,2,0,1:T(8,128)S(1)}, f32[3,1,64,64]{3,2,0,1:T(8,128)}, u32[]{:S(2)}) copy-start(f32[3,1,64,64]{3,2,0,1:T(8,128)} %convolution_bitcast_fusion.22) | copy-start | bytes 147460
  134.1 7.1 %copy-start.87 = (f32[3,1,64,64]{3,2,0,1:T(8,128)S(1)}, f32[3,1,64,64]{3,2,0,1:T(8,128)}, u32[]{:S(2)}) copy-start(f32[3,1,64,64]{3,2,0,1:T(8,128)} %convolution_bitcast_fusion.21) | copy-start | bytes 147460
  134.5 6.6 %copy-start.90 = (f32[3,1,64,64]{3,2,0,1:T(8,128)S(1)}, f32[3,1,64,64]{3,2,0,1:T(8,128)}, u32[]{:S(2)}) copy-start(f32[3,1,64,64]{3,2,0,1:T(8,128)} %convolution_bitcast_fusion.18) | copy-start | bytes 147460
  136.7 13.4 %all-to-all-start.2 = ((bf16[16,2,1024]{2,1,0:T(2,128)(2,1)}), bf16[16,2,1024]{2,1,0:T(2,128)(2,1)S(1)}, u32[]{:S(2)}, u32[]{:S(2)}) async-start(bf16[16,2,1024]{2,1,0:T(2,128)(2,1)} %reshape.405), calls=%async_computation.2 | async-start | bytes 131072 | tf_op jit(solution)/shard_map/all_to_all | solution.py:70
  141.1 263.8 %all-reduce.4.cloned.1.call-start = ((), (), s32[]{:S(2)}) async-start(), calls=%async_computation.7 | async-start | bytes 1769472 | tf_op jit(solution)/shard_map/psum | solution.py:194
  142.3 362.8 %reduce-scatter.2.cloned.1.call-start = ((), (), s32[]{:S(2)}) async-start(), calls=%async_computation.6 | async-start | bytes 6684672 | tf_op jit(solution)/shard_map/reduce_scatter | solution.py:169
  159.6 17.6 %collective-permute-start.2 = (bf16[64,1,1024]{0,2,1:T(8,128)(2,1)S(1)}, bf16[64,1,1024]{0,2,1:T(8,128)(2,1)S(1)}, u32[]{:S(2)}, u32[]{:S(2)}) collective-permute-start(bf16[64,1,1024]{0,2,1:T(8,128)(2,1)S(1)} %get-tuple-element.66), channel_id=1, source_target_pairs={{0,1},{1,2},{2,3},{3,4},{4,5},{5,6},{6,7},{7,8},{8,9},{9,10},{10,1... | collective-permute-start | bytes 393224 | tf_op jit(solution)/shard_map/ppermute | solution.py:24
  162.2 15.0 %collective-permute-start.3 = (bf16[64,1,1024]{0,2,1:T(8,128)(2,1)S(1)}, bf16[64,1,1024]{0,2,1:T(8,128)(2,1)S(1)}, u32[]{:S(2)}, u32[]{:S(2)}) collective-permute-start(bf16[64,1,1024]{0,2,1:T(8,128)(2,1)S(1)} %get-tuple-element.67), channel_id=1, source_target_pairs={{1,0},{2,1},{3,2},{4,3},{5,4},{6,5},{7,6},{8,7},{9,8},{10,9},{11,1... | collective-permute-start | bytes 393224 | tf_op jit(solution)/shard_map/ppermute | solution.py:26
  170.8 236.3 %all-to-all-start.3 = ((bf16[16,2,1024]{2,1,0:T(2,128)(2,1)}), bf16[16,2,1024]{2,1,0:T(2,128)(2,1)S(1)}, u32[]{:S(2)}, u32[]{:S(2)}) async-start(bf16[16,2,1024]{2,1,0:T(2,128)(2,1)} %reshape.407), calls=%async_computation.3 | async-start | bytes 131072 | tf_op jit(solution)/shard_map/all_to_all | solution.py:74
  192.8 13.0 %copy-start.10 = (bf16[64,2,32,32]{0,3,2,1:T(8,128)(2,1)S(1)}, bf16[64,2,32,32]{0,3,2,1:T(8,128)(2,1)}, u32[]{:S(2)}) copy-start(bf16[64,2,32,32]{0,3,2,1:T(8,128)(2,1)} %get-tuple-element.23) | copy-start | bytes 786436
  194.1 12.6 %copy-start.8 = (bf16[64,2,32,32]{0,3,2,1:T(8,128)(2,1)S(1)}, bf16[64,2,32,32]{0,3,2,1:T(8,128)(2,1)}, u32[]{:S(2)}) copy-start(bf16[64,2,32,32]{0,3,2,1:T(8,128)(2,1)} %get-tuple-element.24) | copy-start | bytes 786436
  206.7 11.6 %copy-start.6 = (bf16[64,2,32,32]{0,3,2,1:T(8,128)(2,1)S(1)}, bf16[64,2,32,32]{0,3,2,1:T(8,128)(2,1)}, u32[]{:S(2)}) copy-start(bf16[64,2,32,32]{0,3,2,1:T(8,128)(2,1)} %get-tuple-element.31) | copy-start | bytes 786436
  207.6 11.6 %copy-start.4 = (bf16[64,2,32,32]{0,3,2,1:T(8,128)(2,1)S(1)}, bf16[64,2,32,32]{0,3,2,1:T(8,128)(2,1)}, u32[]{:S(2)}) copy-start(bf16[64,2,32,32]{0,3,2,1:T(8,128)(2,1)} %get-tuple-element.32) | copy-start | bytes 786436
  218.3 3.6 copy-start.14
  219.2 4.2 copy-start.17
  220.1 3.3 copy-start.61
  221.9 4.9 copy-start.67
  221.9 4.9 copy-start.68
  221.9 4.9 copy-start.69
  223.4 4.6 copy-start.70
  223.4 4.6 copy-start.71
  223.4 4.6 copy-start.72
  224.6 4.6 copy-start.73
  224.6 4.6 copy-start.74
  224.6 4.6 copy-start.75
  226.9 3.4 copy-start.76
  226.9 3.4 copy-start.77
  226.9 3.4 copy-start.79
  228.0 3.4 copy-start.43
  228.0 3.4 copy-start.46
  228.0 3.4 copy-start.78
  (38 other events, 75.5 us)
Sparse Core Ops, SparseCore 0:
  10.7 71.3 all-gather.1
  148.0 256.8 all-reduce.3
  409.9 95.1 reduce-scatter.1
where the time goes:
time: 520 us; the launch traced here: 514 us
  waiting for transfers between devices  281 us (54%)
  local copies, waits for them, and re-layouts  117 us (22%)
  matrix products  47.2 us (9%)
  starting transfers between devices  36.8 us (7%)
  other arithmetic  17.1 us (3%)
  between operations  15.2 us (3%)
    psum x1, waiting for transfers between devices, shards(): kernel_total = lax.psum(kernel_local, ('batch', 'space'))  172 us
    reduce_scatter x1, waiting for transfers between devices, shards(): lax.psum_scatter(jnp.einsum('ipxy,opxy->xypio', coef, mixed_grad, preferr...  92.8 us
    another operation x53, local copies, waits for them, and re-layouts, stacked_window(): jnp.stack([window[:, offset_z:offset_z + depth_cells] for offset_z in ran...  76.6 us
    dot_general x18, matrix products, stencil(): lax.dot_general(kernel[:, offset_x, offset_y], stacked, (((0, 1), (0, 1))...  22.9 us
    all_to_all x2, starting transfers between devices, to_pencils(): lax.all_to_all(values, 'space', split_axis=3, concat_axis=1, tiled=True)  15.8 us
    all_to_all x2, starting transfers between devices, to_slabs(): lax.all_to_all(values, 'space', split_axis=1, concat_axis=3, tiled=True)  11.5 us
    all_to_all x2, waiting for transfers between devices, to_pencils(): lax.all_to_all(values, 'space', split_axis=3, concat_axis=1, tiled=True)  11.2 us
    slice x4, local copies, waits for them, and re-layouts, stacked_window(): window[:, offset_z:offset_z + depth_cells]  10.7 us
  transfers between devices with their start and end apart: 11, of which 5 were waited for; matrix products, arithmetic and copies ran while one was open for 30% of the time, Pallas kernels for 0%

commit v1 on v0

--- a/solution.py
+++ b/solution.py
@@ -1,3 +1,4 @@
+import functools
 import math
 import jax
 import jax.numpy as jnp
@@ -11,6 +12,15 @@
 NY = 32
 inv_root_two = 1.0 / math.sqrt(2.0)
 inv_root_two_pi = 1.0 / math.sqrt(2.0 * math.pi)
+
+
+def trace_tiles(local, chip_axis, lane_axis):
+    for to_i in (chip_axis, lane_axis):
+        local = lax.psum(local, to_i)
+    return local
+
+
+lay_results_in = functools.partial(trace_tiles, chip_axis="batch", lane_axis="space")
 
 
 def extended_2(cells, sides, width):
@@ -191,7 +201,7 @@
         .reshape(channels, depth_cells, plane)
     )
     kernel_local = kernel_terms(padded, pre_grad)
-    kernel_total = lax.psum(kernel_local, ("batch", "space"))
+    kernel_total = lay_results_in(kernel_local)
     conv_gradient = kernel_total / math.sqrt(lax.axis_size("batch") * total_depth * plane)
     return (activated[None], input_gradient[None], mode_gradient, conv_gradient)
 

time: 520 us -> 553 us (1.063)
  waiting for transfers between devices: 281 us -> 310 us
    psum x1 -> x2, waiting for transfers between devices: 172 us -> 195 us  [trace_tiles(): local = lax.psum(local, to_i)]
    reduce_scatter x1, waiting for transfers between devices: 92.8 us -> 99.1 us  [shards(): lax.psum_scatter(jnp.einsum('ipxy,opxy->xypio', coef, mixed_grad, preferr...]
  transfers between devices with their start and end apart: 11 -> 12, of which waited for: 5 -> 6; matrix products, arithmetic and copies ran while one was open for 30% -> 28% of each run, Pallas kernels for 0% -> 0%
where the time goes in v1:
time: 553 us; the launch traced here: 547 us
  waiting for transfers between devices  310 us (56%)
  local copies, waits for them, and re-layouts  116 us (21%)
  matrix products  47.2 us (9%)
  starting transfers between devices  41.7 us (8%)
  other arithmetic  17.1 us (3%)
  between operations  15.2 us (3%)
    psum x2, waiting for transfers between devices, trace_tiles(): local = lax.psum(local, to_i)  195 us
    reduce_scatter x1, waiting for transfers between devices, shards(): lax.psum_scatter(jnp.einsum('ipxy,opxy->xypio', coef, mixed_grad, preferr...  99.1 us
    another operation x53, local copies, waits for them, and re-layouts, stacked_window(): jnp.stack([window[:, offset_z:offset_z + depth_cells] for offset_z in ran...  76.4 us
    dot_general x18, matrix products, stencil(): lax.dot_general(kernel[:, offset_x, offset_y], stacked, (((0, 1), (0, 1))...  22.9 us
    all_to_all x2, starting transfers between devices, to_pencils(): lax.all_to_all(values, 'space', split_axis=3, concat_axis=1, tiled=True)  15.8 us
    all_to_all x2, starting transfers between devices, to_slabs(): lax.all_to_all(values, 'space', split_axis=1, concat_axis=3, tiled=True)  15.8 us
    all_to_all x2, waiting for transfers between devices, to_pencils(): lax.all_to_all(values, 'space', split_axis=3, concat_axis=1, tiled=True)  11.2 us
  transfers between devices with their start and end apart: 12, of which 6 were waited for; matrix products, arithmetic and copies ran while one was open for 28% of the time, Pallas kernels for 0%

profile of v1, /device:TPU:2, one launch (start us, length us, event | category | flops | bytes accessed | tf_op | source)
XLA Modules:
  0.0 547.0 jit_solution(1824815242478243762)
XLA Ops:
  10.0 4.2 collective-permute-start
  15.5 1.8 reshape_squeeze.4
  17.3 2.2 fusion.6
  19.5 3.6 convert_element_type.165
  25.6 1.8 copy.99
  28.2 11.5 %all-to-all-start = ((bf16[16,2,1024]{2,1,0:T(2,128)(2,1)}), bf16[16,2,1024]{2,1,0:T(2,128)(2,1)S(1)}, u32[]{:S(2)}, u32[]{:S(2)}) async-start(bf16[16,2,1024]{2,1,0:T(2,128)(2,1)} %reshape.401), calls=%async_computation | async-start | bytes 131072 | tf_op jit(solution)/shard_map/all_to_all | solution.py:80
  40.6 1.8 copy.190
  42.4 2.9 convert_element_type.178
  45.3 3.4 all-to-all-done
  53.0 1.6 select_maximum_fusion.2
  54.5 1.5 fusion.196
  56.0 1.9 copy.109
  58.0 1.9 copy.107
  61.7 3.9 fusion.195
  65.6 2.0 copy.134
  67.6 2.0 copy.133
  69.6 1.9 copy.132
  71.5 1.9 copy.130
  73.5 1.9 copy.129
  75.4 1.9 copy.128
  77.4 1.9 copy.126
  81.1 2.0 copy.119
  83.1 2.0 copy.118
  85.1 1.9 copy.117
  87.0 1.9 copy.115
  88.9 1.9 copy.114
  93.6 1.4 convolution_bitcast_fusion.17
  95.1 1.5 fusion.19
  99.3 4.6 fusion.3
  105.0 5.2 all-to-all-start.1
  110.3 2.4 fusion.13
  115.4 3.9 all-to-all-done.1
  122.0 2.6 fusion.85
  124.6 2.1 convolution_bitcast_fusion.25
  136.7 4.3 all-to-all-start.2
  142.3 7.8 %all-to-all-done.2 = bf16[16,2,1024]{2,1,0:T(2,128)(2,1)S(1)} async-done(((bf16[16,2,1024]{2,1,0:T(2,128)(2,1)}), bf16[16,2,1024]{2,1,0:T(2,128)(2,1)S(1)}, u32[]{:S(2)}, u32[]{:S(2)}) %all-to-all-start.2) | async-done | bytes 65568 | tf_op jit(solution)/shard_map/all_to_all | solution.py:80
  150.6 134.2 %all-reduce.5.cloned.1.call-done = f32[3,3,3,64,64]{4,3,0,2,1:T(8,128)} async-done(((f32[3,3,3,64,64]{4,3,0,2,1:T(8,128)}), f32[3,3,3,64,64]{4,3,0,2,1:T(8,128)}) %all-reduce.5.cloned.1.call-update) | async-done | bytes 442384 | tf_op jit(solution)/shard_map/psum | solution.py:19
  284.9 5.8 %fusion = bf16[16,1,24,64,64]{4,3,2,1,0:T(8,128)(2,1)} fusion(f32[16,24,64]{2,1,0:T(8,128)S(1)} %get-tuple-element.76, f32[16,24,64]{2,1,0:T(8,128)S(1)} %get-tuple-element.77), kind=kLoop, calls=%fused_computation.1 | loop fusion | flops 3145728 | bytes 3342336 | tf_op jit(solution)/shard_map/convert_element_type | solution.py:180
  293.8 3.1 collective-permute-start.2
  296.9 1.3 collective-permute-start.3
  298.2 6.1 %fusion.1 = bf16[24,16,1,64]{3,2,1,0:T(2,128)(2,1)S(1)} fusion(bf16[64,24,16,1]{0,1,2,3:T(8,128)(2,1)S(1)} %bitcast.459, bf16[16,1,24,64,64]{4,3,2,1,0:T(8,128)(2,1)} %all-gather.2.cloned.1.call-done), kind=kOutput, calls=%fused_computation.4 | convolution fusion | flops 3145728 | bytes 3244032 | tf_op jit(solution)/shard_map/opxy,xypio->ipxy/dot_general | solution.py:176
  305.5 10.6 %all-to-all-start.3 = ((bf16[16,2,1024]{2,1,0:T(2,128)(2,1)}), bf16[16,2,1024]{2,1,0:T(2,128)(2,1)S(1)}, u32[]{:S(2)}, u32[]{:S(2)}) async-start(bf16[16,2,1024]{2,1,0:T(2,128)(2,1)} %reshape.407), calls=%async_computation.3 | async-start | bytes 131072 | tf_op jit(solution)/shard_map/all_to_all | solution.py:84
  318.2 1.6 select_maximum_fusion
  319.8 1.4 fusion.194
  321.3 1.9 copy.148
  323.2 1.9 copy.152
  327.8 3.8 fusion.193
  333.0 2.0 copy.172
  335.0 1.9 copy.171
  336.9 1.9 copy.170
  338.8 1.9 copy.169
  340.8 1.9 copy.168
  342.7 1.9 copy.167
  346.4 2.0 copy.164
  348.5 1.9 copy.163
  350.4 1.9 copy.162
  352.3 1.9 copy.159
  354.3 1.9 copy.158
  360.8 1.4 convolution_bitcast_fusion.4
  363.4 2.3 convolution_bitcast_fusion.1
  373.2 2.4 fusion.30
  376.5 60.5 %all-reduce.7.cloned.1.call-done = f32[3,3,3,64,64]{4,3,0,2,1:T(8,128)} async-done(((f32[3,3,3,64,64]{4,3,0,2,1:T(8,128)}), f32[3,3,3,64,64]{4,3,0,2,1:T(8,128)}) %all-reduce.7.cloned.1.call-update) | async-done | bytes 442384 | tf_op jit(solution)/shard_map/psum | solution.py:19
  439.2 99.1 %reduce-scatter.2.cloned.1.call-done = bf16[1,1,24,64,64]{4,3,2,1,0:T(8,128)(2,1)} async-done(((bf16[16,1,24,64,64]{4,3,2,1,0:T(8,128)(2,1)}), bf16[1,1,24,64,64]{4,3,2,1,0:T(8,128)(2,1)}) %reduce-scatter.2.cloned.1.call-update) | async-done | bytes 196624 | tf_op jit(solution)/shard_map/reduce_scatter | solution.py:179
  538.3 2.0 convert_element_type.196
  (296 shorter events, 67.9 us)
Async XLA Ops:
  7.2 92.1 %all-gather.2.cloned.1.call-start = ((), (), s32[]{:S(2)}) async-start(), calls=%async_computation.5 | async-start | bytes 6684672 | tf_op jit(solution)/shard_map/all_gather | solution.py:145
  10.0 40.0 %collective-permute-start = (bf16[64,1,1024]{0,2,1:T(8,128)(2,1)}, bf16[64,1,1024]{0,2,1:T(8,128)(2,1)}, u32[]{:S(2)}, u32[]{:S(2)}) collective-permute-start(bf16[64,1,1024]{0,2,1:T(8,128)(2,1)} %get-tuple-element.72), channel_id=1, source_target_pairs={{0,1},{1,2},{2,3},{3,4},{4,5},{5,6},{6,7},{7,8},{8,9},{9,10},{10,1... | collective-permute-start | bytes 393224 | tf_op jit(solution)/shard_map/ppermute | solution.py:34
  14.2 35.8 %collective-permute-start.1 = (bf16[64,1,1024]{0,2,1:T(8,128)(2,1)}, bf16[64,1,1024]{0,2,1:T(8,128)(2,1)}, u32[]{:S(2)}, u32[]{:S(2)}) collective-permute-start(bf16[64,1,1024]{0,2,1:T(8,128)(2,1)} %get-tuple-element.73), channel_id=1, source_target_pairs={{1,0},{2,1},{3,2},{4,3},{5,4},{6,5},{7,6},{8,7},{9,8},{10,9},{11,1... | collective-permute-start | bytes 393224 | tf_op jit(solution)/shard_map/ppermute | solution.py:36
  19.5 20.2 %copy-start.1 = (bf16[1,64,2,1024]{3,2,1,0:T(2,128)(2,1)S(1)}, bf16[1,64,2,1024]{3,2,1,0:T(2,128)(2,1)}, u32[]{:S(2)}) copy-start(bf16[1,64,2,1024]{3,2,1,0:T(2,128)(2,1)} %param.4) | copy-start | bytes 786436
  28.2 20.6 %all-to-all-start = ((bf16[16,2,1024]{2,1,0:T(2,128)(2,1)}), bf16[16,2,1024]{2,1,0:T(2,128)(2,1)S(1)}, u32[]{:S(2)}, u32[]{:S(2)}) async-start(bf16[16,2,1024]{2,1,0:T(2,128)(2,1)} %reshape.401), calls=%async_computation | async-start | bytes 131072 | tf_op jit(solution)/shard_map/all_to_all | solution.py:80
  65.6 13.7 %copy-start.9 = (bf16[64,2,32,32]{0,3,2,1:T(8,128)(2,1)S(1)}, bf16[64,2,32,32]{0,3,2,1:T(8,128)(2,1)}, u32[]{:S(2)}) copy-start(bf16[64,2,32,32]{0,3,2,1:T(8,128)(2,1)} %get-tuple-element.49) | copy-start | bytes 786436
  67.6 12.6 %copy-start.7 = (bf16[64,2,32,32]{0,3,2,1:T(8,128)(2,1)S(1)}, bf16[64,2,32,32]{0,3,2,1:T(8,128)(2,1)}, u32[]{:S(2)}) copy-start(bf16[64,2,32,32]{0,3,2,1:T(8,128)(2,1)} %get-tuple-element.50) | copy-start | bytes 786436
  80.2 11.6 %copy-start.5 = (bf16[64,2,32,32]{0,3,2,1:T(8,128)(2,1)S(1)}, bf16[64,2,32,32]{0,3,2,1:T(8,128)(2,1)}, u32[]{:S(2)}) copy-start(bf16[64,2,32,32]{0,3,2,1:T(8,128)(2,1)} %get-tuple-element.57) | copy-start | bytes 786436
  81.1 11.6 %copy-start.3 = (bf16[64,2,32,32]{0,3,2,1:T(8,128)(2,1)S(1)}, bf16[64,2,32,32]{0,3,2,1:T(8,128)(2,1)}, u32[]{:S(2)}) copy-start(bf16[64,2,32,32]{0,3,2,1:T(8,128)(2,1)} %get-tuple-element.58) | copy-start | bytes 786436
  83.1 10.5 %copy-start.22 = (bf16[1,64,2048]{2,1,0:T(8,128)(2,1)S(1)}, bf16[1,64,2048]{2,1,0:T(8,128)(2,1)}, u32[]{:S(2)}) copy-start(bf16[1,64,2048]{2,1,0:T(8,128)(2,1)} %copy.107) | copy-start | bytes 786436
  91.8 3.3 copy-start.19
  92.7 3.9 copy-start.55
  92.7 3.9 copy-start.57
  93.6 3.3 copy-start.49
  93.6 3.3 copy-start.51
  93.6 3.4 copy-start.53
  99.3 11.0 %copy-start.30 = (bf16[1,64,2048]{2,1,0:T(8,128)(2,1)S(1)}, bf16[1,64,2048]{2,1,0:T(8,128)(2,1)}, u32[]{:S(2)}) copy-start(bf16[1,64,2048]{2,1,0:T(8,128)(2,1)} %copy.134) | copy-start | bytes 786436
  99.3 11.0 %copy-start.32 = (bf16[1,64,2048]{2,1,0:T(8,128)(2,1)S(1)}, bf16[1,64,2048]{2,1,0:T(8,128)(2,1)}, u32[]{:S(2)}) copy-start(bf16[1,64,2048]{2,1,0:T(8,128)(2,1)} %copy.133) | copy-start | bytes 786436
  103.9 9.7 %copy-start.2 = (bf16[64,2,32,32]{0,3,2,1:T(8,128)(2,1)S(1)}, bf16[64,2,32,32]{0,3,2,1:T(8,128)(2,1)}, u32[]{:S(2)}) copy-start(bf16[64,2,32,32]{0,3,2,1:T(8,128)(2,1)} %get-tuple-element.40) | copy-start | bytes 786436
  105.0 14.3 %all-to-all-start.1 = ((bf16[16,2,1024]{2,1,0:T(2,128)(2,1)}), bf16[16,2,1024]{2,1,0:T(2,128)(2,1)}, u32[]{:S(2)}, u32[]{:S(2)}) async-start(bf16[16,2,1024]{2,1,0:T(2,128)(2,1)} %reshape.403), calls=%async_computation.1 | async-start | bytes 131072 | tf_op jit(solution)/shard_map/all_to_all | solution.py:84
  110.3 11.3 %copy-start = (bf16[256,1024]{1,0:T(8,128)(2,1)S(1)}, bf16[256,1024]{1,0:T(8,128)(2,1)}, u32[]{:S(2)}) copy-start(bf16[256,1024]{1,0:T(8,128)(2,1)} %convert_element_type.178) | copy-start | bytes 1572868
  113.5 8.5 %copy-start.18 = (f32[8,8,2,1024]{3,1,2,0:T(8,128)S(1)}, f32[8,8,2,1024]{3,1,2,0:T(8,128)}, u32[]{:S(2)}) copy-start(f32[8,8,2,1024]{3,1,2,0:T(8,128)} %copy.190) | copy-start | bytes 1572868
  122.0 4.7 copy-start.56
  122.0 4.7 copy-start.58
  122.0 4.7 copy-start.60
  124.6 168.0 %copy-start.13 = (bf16[64,2048]{1,0:T(8,128)(2,1)}, bf16[64,2048]{1,0:T(8,128)(2,1)S(1)}, u32[]{:S(2)}) copy-start(bf16[64,2048]{1,0:T(8,128)(2,1)S(1)} %get-tuple-element.68) | copy-start | bytes 786436
  124.6 3.2 copy-start.54
  134.0 7.0 %copy-start.88 = (f32[3,1,64,64]{3,2,0,1:T(8,128)S(1)}, f32[3,1,64,64]{3,2,0,1:T(8,128)}, u32[]{:S(2)}) copy-start(f32[3,1,64,64]{3,2,0,1:T(8,128)} %convolution_bitcast_fusion.20) | copy-start | bytes 147460
  134.0 7.0 %copy-start.89 = (f32[3,1,64,64]{3,2,0,1:T(8,128)S(1)}, f32[3,1,64,64]{3,2,0,1:T(8,128)}, u32[]{:S(2)}) copy-start(f32[3,1,64,64]{3,2,0,1:T(8,128)} %convolution_bitcast_fusion.19) | copy-start | bytes 147460
  134.0 7.1 %copy-start.83 = (f32[3,1,64,64]{3,2,0,1:T(8,128)S(1)}, f32[3,1,64,64]{3,2,0,1:T(8,128)}, u32[]{:S(2)}) copy-start(f32[3,1,64,64]{3,2,0,1:T(8,128)} %convolution_bitcast_fusion.25) | copy-start | bytes 147460
  134.0 7.1 %copy-start.84 = (f32[3,1,64,64]{3,2,0,1:T(8,128)S(1)}, f32[3,1,64,64]{3,2,0,1:T(8,128)}, u32[]{:S(2)}) copy-start(f32[3,1,64,64]{3,2,0,1:T(8,128)} %convolution_bitcast_fusion.24) | copy-start | bytes 147460
  134.1 7.1 %copy-start.85 = (f32[3,1,64,64]{3,2,0,1:T(8,128)S(1)}, f32[3,1,64,64]{3,2,0,1:T(8,128)}, u32[]{:S(2)}) copy-start(f32[3,1,64,64]{3,2,0,1:T(8,128)} %convolution_bitcast_fusion.23) | copy-start | bytes 147460
  134.1 7.1 %copy-start.86 = (f32[3,1,64,64]{3,2,0,1:T(8,128)S(1)}, f32[3,1,64,64]{3,2,0,1:T(8,128)}, u32[]{:S(2)}) copy-start(f32[3,1,64,64]{3,2,0,1:T(8,128)} %convolution_bitcast_fusion.22) | copy-start | bytes 147460
  134.1 7.1 %copy-start.87 = (f32[3,1,64,64]{3,2,0,1:T(8,128)S(1)}, f32[3,1,64,64]{3,2,0,1:T(8,128)}, u32[]{:S(2)}) copy-start(f32[3,1,64,64]{3,2,0,1:T(8,128)} %convolution_bitcast_fusion.21) | copy-start | bytes 147460
  134.4 6.6 %copy-start.90 = (f32[3,1,64,64]{3,2,0,1:T(8,128)S(1)}, f32[3,1,64,64]{3,2,0,1:T(8,128)}, u32[]{:S(2)}) copy-start(f32[3,1,64,64]{3,2,0,1:T(8,128)} %convolution_bitcast_fusion.18) | copy-start | bytes 147460
  136.7 13.4 %all-to-all-start.2 = ((bf16[16,2,1024]{2,1,0:T(2,128)(2,1)}), bf16[16,2,1024]{2,1,0:T(2,128)(2,1)S(1)}, u32[]{:S(2)}, u32[]{:S(2)}) async-start(bf16[16,2,1024]{2,1,0:T(2,128)(2,1)} %reshape.405), calls=%async_computation.2 | async-start | bytes 131072 | tf_op jit(solution)/shard_map/all_to_all | solution.py:80
  141.0 143.8 %all-reduce.5.cloned.1.call-start = ((), (), s32[]{:S(2)}) async-start(), calls=%async_computation.7 | async-start | bytes 1769472 | tf_op jit(solution)/shard_map/psum | solution.py:19
  142.2 294.7 %all-reduce.7.cloned.1.call-start = ((), (), s32[]{:S(2)}) async-start(), calls=%async_computation.8 | async-start | bytes 1769472 | tf_op jit(solution)/shard_map/psum | solution.py:19
  284.8 253.5 %reduce-scatter.2.cloned.1.call-start = ((), (), s32[]{:S(2)}) async-start(), calls=%async_computation.6 | async-start | bytes 6684672 | tf_op jit(solution)/shard_map/reduce_scatter | solution.py:179
  293.8 22.4 %collective-permute-start.2 = (bf16[64,1,1024]{0,2,1:T(8,128)(2,1)S(1)}, bf16[64,1,1024]{0,2,1:T(8,128)(2,1)S(1)}, u32[]{:S(2)}, u32[]{:S(2)}) collective-permute-start(bf16[64,1,1024]{0,2,1:T(8,128)(2,1)S(1)} %get-tuple-element.66), channel_id=1, source_target_pairs={{0,1},{1,2},{2,3},{3,4},{4,5},{5,6},{6,7},{7,8},{8,9},{9,10},{10,1... | collective-permute-start | bytes 393224 | tf_op jit(solution)/shard_map/ppermute | solution.py:34
  296.9 19.3 %collective-permute-start.3 = (bf16[64,1,1024]{0,2,1:T(8,128)(2,1)S(1)}, bf16[64,1,1024]{0,2,1:T(8,128)(2,1)S(1)}, u32[]{:S(2)}, u32[]{:S(2)}) collective-permute-start(bf16[64,1,1024]{0,2,1:T(8,128)(2,1)S(1)} %get-tuple-element.67), channel_id=1, source_target_pairs={{1,0},{2,1},{3,2},{4,3},{5,4},{6,5},{7,6},{8,7},{9,8},{10,9},{11,1... | collective-permute-start | bytes 393224 | tf_op jit(solution)/shard_map/ppermute | solution.py:36
  305.5 65.8 %all-to-all-start.3 = ((bf16[16,2,1024]{2,1,0:T(2,128)(2,1)}), bf16[16,2,1024]{2,1,0:T(2,128)(2,1)S(1)}, u32[]{:S(2)}, u32[]{:S(2)}) async-start(bf16[16,2,1024]{2,1,0:T(2,128)(2,1)} %reshape.407), calls=%async_computation.3 | async-start | bytes 131072 | tf_op jit(solution)/shard_map/all_to_all | solution.py:84
  331.6 13.0 %copy-start.10 = (bf16[64,2,32,32]{0,3,2,1:T(8,128)(2,1)S(1)}, bf16[64,2,32,32]{0,3,2,1:T(8,128)(2,1)}, u32[]{:S(2)}) copy-start(bf16[64,2,32,32]{0,3,2,1:T(8,128)(2,1)} %get-tuple-element.23) | copy-start | bytes 786436
  333.0 12.6 %copy-start.8 = (bf16[64,2,32,32]{0,3,2,1:T(8,128)(2,1)S(1)}, bf16[64,2,32,32]{0,3,2,1:T(8,128)(2,1)}, u32[]{:S(2)}) copy-start(bf16[64,2,32,32]{0,3,2,1:T(8,128)(2,1)} %get-tuple-element.24) | copy-start | bytes 786436
  345.5 11.6 %copy-start.6 = (bf16[64,2,32,32]{0,3,2,1:T(8,128)(2,1)S(1)}, bf16[64,2,32,32]{0,3,2,1:T(8,128)(2,1)}, u32[]{:S(2)}) copy-start(bf16[64,2,32,32]{0,3,2,1:T(8,128)(2,1)} %get-tuple-element.31) | copy-start | bytes 786436
  346.4 11.6 %copy-start.4 = (bf16[64,2,32,32]{0,3,2,1:T(8,128)(2,1)S(1)}, bf16[64,2,32,32]{0,3,2,1:T(8,128)(2,1)}, u32[]{:S(2)}) copy-start(bf16[64,2,32,32]{0,3,2,1:T(8,128)(2,1)} %get-tuple-element.32) | copy-start | bytes 786436
  357.1 3.7 copy-start.14
  358.0 4.2 copy-start.17
  358.9 3.3 copy-start.61
  360.8 4.9 copy-start.67
  360.8 4.9 copy-start.68
  360.8 4.9 copy-start.69
  362.2 4.6 copy-start.70
  362.3 4.6 copy-start.71
  362.3 4.6 copy-start.72
  363.4 4.6 copy-start.73
  363.4 4.6 copy-start.74
  363.4 4.6 copy-start.75
  365.7 3.4 copy-start.76
  365.7 3.4 copy-start.77
  365.7 3.4 copy-start.79
  366.8 3.4 copy-start.43
  366.8 3.3 copy-start.46
  366.8 3.3 copy-start.78
  (39 other events, 78.8 us)
Sparse Core Ops, SparseCore 0:
  10.7 71.3 all-gather.1
  145.1 139.6 all-reduce.4
  287.6 149.2 all-reduce.6
  441.2 97.0 reduce-scatter.1
